TPU v7x, 256 devices: a whole 4x4x8 slice. The times are simulated.
256 devices in a mesh: grp: 4 (over y), tok: 64 (over z, x, core).
Axes of the slice: x: 4, y: 4, z: 8, core: 2. Of those that a mesh axis runs over, the one named last changes fastest.
Arguments:
- hidden: bfloat16 [512, 64, 1024], P('tok', 'grp'), may hold values from -6 to 6
- draft_qkv: bfloat16 [3, 512, 64, 1024], P(None, 'tok', None, 'grp'), may hold values from -4 to 4
- self_cache: bfloat16 [512, 2, 512, 1024], P('tok', None, None, 'grp'), may hold values from -4 to 4
- cross_cache: bfloat16 [512, 2, 512, 1024], P('tok', None, None, 'grp'), may hold values from -4 to 4
- parents: int32 [512, 64], P('tok'), may hold values from -1 to 62, as said below
- counts: int32 [512], P('tok'), may hold values from 32 to 64, as said below
- self_len: int32 [512], P('tok'), may hold values from 2 to 512, as said below
- enc_len: int32 [512], P('tok'), may hold values from 2 to 512, as said below
- buckets: int32 [512, 64, 64], P('tok'), may hold values from 0 to 31
- bias_table: float32 [32, 16], P(None, 'grp'), may hold values from -4 to 4
- gain_cross: float32 [1024], replicated, may hold values from 0.25 to 1.75
- gain_ffn: float32 [1024], replicated, may hold values from 0.25 to 1.75
- gain_next: float32 [1024], replicated, may hold values from 0.25 to 1.75
- w_out_self: bfloat16 [1024, 1024], P('grp', 'tok'), may hold values from -0.1875 to 0.1875
- w_query_cross: bfloat16 [1024, 1024], P('tok', 'grp'), may hold values from -1 to 1
- w_out_cross: bfloat16 [1024, 1024], P('grp', 'tok'), may hold values from -0.1875 to 0.1875
- w_gate: bfloat16 [1024, 2816], P('tok', 'grp'), may hold values from -0.1875 to 0.1875
- w_up: bfloat16 [1024, 2816], P('tok', 'grp'), may hold values from -0.1875 to 0.1875
- w_down: bfloat16 [2816, 1024], P('grp', 'tok'), may hold values from -0.109375 to 0.109375
- w_qkv: bfloat16 [1024, 3, 1024], P('tok', None, 'grp'), may hold values from -0.1875 to 0.1875
Outputs:
- out_hidden: bfloat16 [512, 64, 1024], P('tok', 'grp')
- next_qkv: bfloat16 [3, 512, 64, 1024], P(None, 'tok', None, 'grp')
Inputs may be any that keep to these rules, and one draw needn't show every extreme that they name: `parents`: slot 0 of every tree has parent -1; every other slot's parent is an earlier slot. `counts`: some request fills all 64 draft slots. `self_len`: some request fills its whole cache. `enc_len`: some request has all 512 encoder positions.
All inputs are finite; a program needn't handle non-finite values.
Results may differ from a plain program's by a relative error of at most 0.025.
Values may be sent and summed in bfloat16 or wider, within the bound.
A program may use at most 64 MiB of HBM per device.

v0:
```python
import jax
import jax.numpy as jnp
from jax import lax
from jax.sharding import PartitionSpec as P

DH = 64


def ancestor_table(parent_ids):
    count_slots = parent_ids.shape[0]
    slot_ids = jnp.arange(count_slots, dtype=jnp.int32)
    ancestors = jnp.eye(count_slots, dtype=jnp.float32) + (
        parent_ids[:, None] == slot_ids[None, :]
    ).astype(jnp.float32)
    for repeat in range(max(1, count_slots.bit_length())):
        ancestors = jnp.minimum(jnp.dot(ancestors, ancestors, precision=lax.Precision.HIGHEST), 1.0)
    return ancestors


def rms_scale(stream, gain_vec):
    mean_square = jnp.mean(stream * stream, axis=-1, keepdims=True)
    return (stream * lax.rsqrt(mean_square + 1e-06) * gain_vec).astype(jnp.bfloat16)


def draft_attention(projected, cached, parent_ids, draft_count, length, bucket_ids, bias_table):
    requests, draft_slots, head_width = (projected.shape[1], projected.shape[2], projected.shape[3])
    local_heads = bias_table.shape[1]
    head_size = head_width // local_heads
    queries = projected[0].reshape(requests, draft_slots, local_heads, head_size)
    draft_keys = projected[1].reshape(requests, draft_slots, local_heads, head_size)
    draft_values = projected[2].reshape(requests, draft_slots, local_heads, head_size)
    cache_keys = cached[:, 0].reshape(requests, -1, local_heads, head_size)
    cache_values = cached[:, 1].reshape(requests, -1, local_heads, head_size)
    cache_scores = jnp.einsum(
        "rihd,rphd->rhip", queries, cache_keys, preferred_element_type=jnp.float32
    )
    cache_scores = cache_scores + bias_table[-1][None, :, None, None]
    cache_live = jnp.arange(cache_keys.shape[1], dtype=jnp.int32)[None, :] < length[:, None]
    cache_scores = jnp.where(cache_live[:, None, None, :], cache_scores, -1e30)
    onehot = (bucket_ids[..., None] == jnp.arange(bias_table.shape[0], dtype=jnp.int32)).astype(
        jnp.float32
    )
    draft_bias = jnp.einsum("rijb,bh->rhij", onehot, bias_table, precision=lax.Precision.HIGHEST)
    draft_scores = (
        jnp.einsum("rihd,rjhd->rhij", queries, draft_keys, preferred_element_type=jnp.float32)
        + draft_bias
    )
    ancestors = jax.vmap(ancestor_table)(parent_ids)
    draft_live = (ancestors > 0.5) & (
        jnp.arange(draft_slots, dtype=jnp.int32)[None, None, :] < draft_count[:, None, None]
    )
    draft_scores = jnp.where(draft_live[:, None], draft_scores, -1e30)
    highest = jnp.maximum(cache_scores.max(-1, keepdims=True), draft_scores.max(-1, keepdims=True))
    exp_cache = jnp.exp(cache_scores - highest)
    exp_draft = jnp.exp(draft_scores - highest)
    denominator = exp_cache.sum(-1, keepdims=True) + exp_draft.sum(-1, keepdims=True)
    weights_cache = (exp_cache / denominator).astype(jnp.bfloat16)
    weights_draft = (exp_draft / denominator).astype(jnp.bfloat16)
    attended = jnp.einsum(
        "rhip,rphd->rihd", weights_cache, cache_values, preferred_element_type=jnp.float32
    )
    attended = attended + jnp.einsum(
        "rhij,rjhd->rihd", weights_draft, draft_values, preferred_element_type=jnp.float32
    )
    return attended.astype(jnp.bfloat16).reshape(requests * draft_slots, head_width)


def cross_attention(query_rows, cached, length):
    requests, draft_slots, head_width = query_rows.shape
    local_heads = head_width // DH
    queries = query_rows.reshape(requests, draft_slots, local_heads, DH)
    enc_keys = cached[:, 0].reshape(requests, -1, local_heads, DH)
    enc_values = cached[:, 1].reshape(requests, -1, local_heads, DH)
    scores = jnp.einsum("rihd,rphd->rhip", queries, enc_keys, preferred_element_type=jnp.float32)
    live = jnp.arange(enc_keys.shape[1], dtype=jnp.int32)[None, :] < length[:, None]
    scores = jnp.where(live[:, None, None, :], scores, -1e30)
    highest = scores.max(-1, keepdims=True)
    exp_scores = jnp.exp(scores - highest)
    weights = (exp_scores / exp_scores.sum(-1, keepdims=True)).astype(jnp.bfloat16)
    attended = jnp.einsum(
        "rhip,rphd->rihd", weights, enc_values, preferred_element_type=jnp.float32
    )
    return attended.astype(jnp.bfloat16).reshape(requests * draft_slots, head_width)


def layer_sum(summand, base_full):
    return lax.psum(summand.astype(jnp.bfloat16), "grp").astype(jnp.float32) + base_full


def normed_rows(stream, gain_vec):
    scaled = rms_scale(stream, gain_vec)
    return scaled.reshape(-1, scaled.shape[-1])


def shards(
    hidden,
    draft_qkv,
    self_cache,
    cross_cache,
    parents,
    counts,
    self_len,
    enc_len,
    buckets,
    bias_table,
    gain_cross,
    gain_ffn,
    gain_next,
    w_out_self,
    w_query_cross,
    w_out_cross,
    w_gate,
    w_up,
    w_down,
    w_qkv,
):
    requests, share_rows, model_width = hidden.shape
    draft_slots = draft_qkv.shape[2]
    head_width = draft_qkv.shape[3]
    fetched = (
        lax.all_gather(w_out_self, "tok", axis=1, tiled=True),
        lax.all_gather(w_query_cross, "tok", axis=0, tiled=True),
        lax.all_gather(w_out_cross, "tok", axis=1, tiled=True),
        lax.all_gather(w_gate, "tok", axis=0, tiled=True),
        lax.all_gather(w_up, "tok", axis=0, tiled=True),
        lax.all_gather(w_down, "tok", axis=1, tiled=True),
        lax.all_gather(w_qkv, "tok", axis=0, tiled=True),
    )
    self_context = draft_attention(
        draft_qkv, self_cache, parents, counts, self_len, buckets, bias_table
    )
    partial_value = jnp.dot(self_context, fetched[0], preferred_element_type=jnp.float32)
    partial_value = partial_value.reshape(requests, draft_slots, model_width)
    own_rows = hidden.astype(jnp.float32)
    offset = lax.axis_index("grp") * share_rows
    placed = lax.dynamic_update_slice(
        jnp.zeros((requests, draft_slots, model_width), jnp.float32), own_rows, (0, offset, 0)
    )
    stream_one = layer_sum(partial_value + placed, 0.0)
    normed_one = normed_rows(stream_one, gain_cross)
    cross_query = jnp.dot(normed_one, fetched[1], preferred_element_type=jnp.float32)
    cross_query = cross_query.astype(jnp.bfloat16).reshape(requests, draft_slots, head_width)
    cross_context = cross_attention(cross_query, cross_cache, enc_len)
    partial_value = jnp.dot(cross_context, fetched[2], preferred_element_type=jnp.float32)
    stream_two = layer_sum(partial_value.reshape(requests, draft_slots, model_width), stream_one)
    normed_two = normed_rows(stream_two, gain_ffn)
    gate_part = jnp.dot(normed_two, fetched[3], preferred_element_type=jnp.float32)
    up_part = jnp.dot(normed_two, fetched[4], preferred_element_type=jnp.float32)
    gated = (jax.nn.gelu(gate_part, approximate=True) * up_part).astype(jnp.bfloat16)
    partial_value = jnp.dot(gated, fetched[5], preferred_element_type=jnp.float32)
    stream_three = layer_sum(partial_value.reshape(requests, draft_slots, model_width), stream_two)
    normed_three = normed_rows(stream_three, gain_next)
    projected = jnp.dot(
        normed_three,
        fetched[6].reshape(fetched[6].shape[0], -1),
        preferred_element_type=jnp.float32,
    )
    projected = projected.astype(jnp.bfloat16).reshape(requests, draft_slots, 3, head_width)
    next_qkv = jnp.transpose(projected, (2, 0, 1, 3))
    out_hidden = lax.dynamic_slice_in_dim(stream_three, offset, share_rows, 1).astype(jnp.bfloat16)
    return (out_hidden, next_qkv)


def solution(mesh):
    in_specs = (
        P("tok", "grp", None),
        P(None, "tok", None, "grp"),
        P("tok", None, None, "grp"),
        P("tok", None, None, "grp"),
        P("tok", None),
        P("tok"),
        P("tok"),
        P("tok"),
        P("tok", None, None),
        P(None, "grp"),
        P(),
        P(),
        P(),
        P("grp", "tok"),
        P("tok", "grp"),
        P("grp", "tok"),
        P("tok", "grp"),
        P("tok", "grp"),
        P("grp", "tok"),
        P("tok", None, "grp"),
    )
    out_specs = (P("tok", "grp", None), P(None, "tok", None, "grp"))
    return jax.shard_map(shards, mesh=mesh, in_specs=in_specs, out_specs=out_specs, check_vma=False)
```

profile of v0, /device:TPU:1, one launch (start us, length us, event | category | flops | bytes accessed | tf_op | source)
XLA Modules:
  0.0 532.7 jit_solution(6397232074818495033)
XLA Ops:
  8.1 3.9 fusion.56
  12.0 2.4 copy.53
  14.6 2.9 copy.47
  17.5 1.9 fusion.57
  19.4 0.2 reshape_squeeze.21
  19.7 3.6 fusion.1
  23.3 2.6 copy.52
  25.8 1.2 reshape_squeeze.23
  27.1 0.5 convolution_minimum_fusion.6
  27.6 0.4 convolution_minimum_fusion.5
  28.0 0.4 convolution_minimum_fusion.4
  28.4 0.4 convolution_minimum_fusion.3
  28.8 0.4 convolution_minimum_fusion.2
  29.2 0.4 convolution_minimum_fusion.1
  29.7 0.4 fusion.29
  30.3 0.8 fusion.3
  31.0 0.4 copy-done.3
  31.5 0.4 fusion.58
  32.0 1.5 fusion.7
  33.7 1.0 reshape_squeeze.25
  34.7 3.0 fusion.14
  37.8 0.4 fusion.27
  38.2 0.4 copy.56
  38.6 0.3 dot_general.79
  39.0 54.8 %all_gather.21 = bf16[256,1024]{0,1:T(8,128)(2,1)S(1)} all-gather(bf16[256,16]{0,1:T(8,128)(2,1)S(1)} %copy-done.9), channel_id=1, replica_groups=mesh['grp'=4,'tok'=64] {'tok'}, dimensions={1}, use_global_device_ids=true | all-gather | bytes 532480 | tf_op jit(solution)/shard_map/all_gather | solution.py:121
  93.8 0.5 fusion.32
  94.4 1.1 convert_element_type.84
  95.6 3.9 fusion.55
  99.5 2.4 copy.59
  101.9 2.9 copy.57
  104.8 49.2 %all_gather.22 = bf16[1024,256]{1,0:T(8,128)(2,1)S(1)} all-gather(bf16[16,256]{1,0:T(8,128)(2,1)S(1)} %copy-done.10), channel_id=1, replica_groups=mesh['grp'=4,'tok'=64] {'tok'}, dimensions={0}, use_global_device_ids=true | all-gather | bytes 532480 | tf_op jit(solution)/shard_map/all_gather | solution.py:122
  154.0 48.2 %all_gather.23 = bf16[256,1024]{0,1:T(8,128)(2,1)S(1)} all-gather(bf16[256,16]{0,1:T(8,128)(2,1)S(1)} %copy-done.11), channel_id=1, replica_groups=mesh['grp'=4,'tok'=64] {'tok'}, dimensions={1}, use_global_device_ids=true | all-gather | bytes 532480 | tf_op jit(solution)/shard_map/all_gather | solution.py:123
  202.2 1.5 fusion.8
  203.8 1.5 fusion.10
  205.3 0.4 convolution_convert_fusion.3
  205.7 0.2 reshape_reshape.3
  206.0 0.7 fusion.34
  206.7 2.0 fusion.59
  208.7 0.8 fusion.26
  209.4 0.4 copy.60
  209.9 0.3 dot_general.84
  210.2 1.5 convolution_convert_fusion.1
  211.8 0.5 all-gather.5.cloned.1.call-update
  212.4 0.5 all-gather.9.cloned.1.call-update
  213.0 0.5 all-gather.7.cloned.1.call-update
  213.6 0.7 all-gather.11.cloned.1.call-update
  214.3 0.3 all-reduce.8.cloned.1.call-start
  214.6 44.3 %all-reduce.6.cloned.1.call-done = bf16[8,64,1024]{2,1,0:T(8,128)(2,1)} async-done(((bf16[8,64,1024]{2,1,0:T(8,128)(2,1)}), bf16[8,64,1024]{2,1,0:T(8,128)(2,1)}) %all-reduce.6.cloned.1.call-update) | async-done | bytes 1048592 | tf_op jit(solution)/shard_map/psum | solution.py:87
  258.9 1.7 multiply_reduce_fusion.1
  260.6 0.4 multiply_convert_fusion.1
  261.0 28.7 %all-gather.5.cloned.1.call-done = bf16[1024,704]{1,0:T(8,128)(2,1)} async-done(((bf16[16,704]{1,0:T(8,128)(2,1)}), bf16[1024,704]{1,0:T(8,128)(2,1)}) %all-gather.5.cloned.1.call-update) | async-done | bytes 1441808 | tf_op jit(solution)/shard_map/all_gather | solution.py:124
  289.7 3.5 fusion.60
  293.2 73.9 %all-gather.9.cloned.1.call-done = bf16[704,1024]{0,1:T(8,128)(2,1)} async-done(((bf16[704,16]{0,1:T(8,128)(2,1)}), bf16[704,1024]{0,1:T(8,128)(2,1)}) %all-gather.9.cloned.1.call-update) | async-done | bytes 1441808 | tf_op jit(solution)/shard_map/all_gather | solution.py:126
  367.1 77.4 %all-gather.7.cloned.1.call-done = bf16[1024,704]{1,0:T(8,128)(2,1)} async-done(((bf16[16,704]{1,0:T(8,128)(2,1)}), bf16[1024,704]{1,0:T(8,128)(2,1)}) %all-gather.7.cloned.1.call-update) | async-done | bytes 1441808 | tf_op jit(solution)/shard_map/all_gather | solution.py:125
  444.5 5.5 %convolution_convert_fusion = bf16[512,1024]{1,0:T(8,128)(2,1)} fusion(bf16[704,1024]{0,1:T(8,128)(2,1)} %all-gather.9.cloned.1.call-done, bf16[512,1024]{1,0:T(8,128)(2,1)S(1)} %bitcast.67, bf16[1024,704]{1,0:T(8,128)(2,1)} %all-gather.7.cloned.1.call-done, f32[512,704]{0,1:T(8,128)} %fusion.60), kind=kOutput, calls=%fused_computation.29 | convolution fusion | flops 1480523776 | bytes 6422528 | tf_op jit(solution)/shard_map/dot_general | solution.py:150
  450.0 67.0 %all-gather.11.cloned.1.call-done = bf16[1024,3,256]{2,0,1:T(8,128)(2,1)} async-done(((bf16[16,3,256]{2,0,1:T(8,128)(2,1)}), bf16[1024,3,256]{2,0,1:T(8,128)(2,1)}) %all-gather.11.cloned.1.call-update) | async-done | bytes 1572880 | tf_op jit(solution)/shard_map/all_gather | solution.py:127
  517.1 2.6 copy.61
  519.7 1.8 multiply_reduce_fusion
  521.4 0.7 dynamic-slice_convert_fusion
  522.2 0.2 multiply_convert_fusion
  522.4 0.5 copy-done.6
  522.9 1.0 convolution_convert_fusion.2
  524.0 0.4 reshape.141
  524.4 1.0 copy.62
  (64 shorter events, 1.3 us)
Async XLA Ops:
  8.0 194.2 %all-reduce.4.cloned.1.call-start = ((), (), s32[]{:S(2)}) async-start(), calls=%async_computation | async-start | bytes 2097152 | tf_op jit(solution)/shard_map/psum | solution.py:87
  12.0 2.4 copy-start.16
  12.0 2.6 copy-start.17
  17.5 2.2 copy-start.19
  19.7 7.4 %copy-start.12 = (s32[8,64]{1,0:T(8,128)S(1)}, s32[8,64]{1,0:T(8,128)}, u32[]{:S(2)}) copy-start(s32[8,64]{1,0:T(8,128)} %param.24) | copy-start | bytes 6148
  27.1 2.5 copy-start.20
  30.3 1.2 copy-start.3
  31.5 2.0 copy-start.1
  31.9 2.8 copy-start.4
  34.7 3.1 copy-start.7
  37.8 1.2 copy-start.9
  38.6 55.7 %copy-start.8 = (bf16[8,16,1024]{2,1,0:T(8,128)(2,1)S(1)}, bf16[8,16,1024]{2,1,0:T(8,128)(2,1)}, u32[]{:S(2)}) copy-start(bf16[8,16,1024]{2,1,0:T(8,128)(2,1)} %param.20) | copy-start | bytes 786436
  95.6 163.3 %all-reduce.6.cloned.1.call-start = ((), (), s32[]{:S(2)}) async-start(), calls=%async_computation.1 | async-start | bytes 2097152 | tf_op jit(solution)/shard_map/psum | solution.py:87
  101.9 2.9 copy-start.10
  101.9 52.1 %copy-start.11 = (bf16[256,16]{0,1:T(8,128)(2,1)S(1)}, bf16[256,16]{0,1:T(8,128)(2,1)}, u32[]{:S(2)}) copy-start(bf16[256,16]{0,1:T(8,128)(2,1)} %param.35) | copy-start | bytes 24580
  101.9 100.3 %copy-start.18 = (s32[8]{0:T(128)S(1)}, s32[8]{0:T(128)}, u32[]{:S(2)}) copy-start(s32[8]{0:T(128)} %param.27) | copy-start | bytes 100
  104.8 98.9 %copy-start.13 = (f32[1024]{0:T(1024)S(1)}, f32[1024]{0:T(1024)}, u32[]{:S(2)}) copy-start(f32[1024]{0:T(1024)} %param.30) | copy-start | bytes 12292
  206.7 2.0 copy-start.5
  209.9 49.0 %copy-start = (bf16[8,64,1024]{2,1,0:T(8,128)(2,1)S(1)}, bf16[8,64,1024]{2,1,0:T(8,128)(2,1)}, u32[]{:S(2)}) copy-start(bf16[8,64,1024]{2,1,0:T(8,128)(2,1)} %all-reduce.4.cloned.1.call-done) | copy-start | bytes 3145732
  210.2 50.4 %copy-start.14 = (f32[1024]{0:T(1024)S(1)}, f32[1024]{0:T(1024)}, u32[]{:S(2)}) copy-start(f32[1024]{0:T(1024)} %param.31) | copy-start | bytes 12292
  211.8 77.9 %all-gather.5.cloned.1.call-start = ((), (), s32[]{:S(2)}) async-start(), calls=%async_computation.2 | async-start | bytes 1597440 | tf_op jit(solution)/shard_map/all_gather | solution.py:124
  212.4 154.7 %all-gather.9.cloned.1.call-start = ((), (), s32[]{:S(2)}) async-start(), calls=%async_computation.4 | async-start | bytes 1597440 | tf_op jit(solution)/shard_map/all_gather | solution.py:126
  213.0 231.5 %all-gather.7.cloned.1.call-start = ((), (), s32[]{:S(2)}) async-start(), calls=%async_computation.3 | async-start | bytes 1597440 | tf_op jit(solution)/shard_map/all_gather | solution.py:125
  213.5 303.5 %all-gather.11.cloned.1.call-start = ((), (), s32[]{:S(2)}) async-start(), calls=%async_computation.6 | async-start | bytes 1597440 | tf_op jit(solution)/shard_map/all_gather | solution.py:127
  214.3 305.4 %all-reduce.8.cloned.1.call-start = ((), (), s32[]{:S(2)}) async-start(), calls=%async_computation.5 | async-start | bytes 2097152 | tf_op jit(solution)/shard_map/psum | solution.py:87
  258.9 1.7 copy-start.2
  519.6 2.5 copy-start.15
  521.4 1.5 copy-start.6
Sparse Core Ops, SparseCore 0:
  95.7 46.8 all-reduce.3
  211.9 46.8 all-reduce.5
  450.1 46.8 all-reduce.7
Sparse Core Ops, SparseCore 1:
  215.0 74.7 all-gather.4
  292.4 74.7 all-gather.8
  369.8 74.7 all-gather.6
  447.5 69.5 all-gather.10
where the time goes:
time: 533 us
  waiting for transfers between devices  294 us (55%)
  blocking collectives  152 us (29%)
  local copies, waits for them, and re-layouts  33.2 us (6%)
  matrix products  25 us (5%)
  between operations  15.9 us (3%)
  other arithmetic  12.3 us (2%)
    all_gather x1, waiting for transfers between devices, shards(): lax.all_gather(w_up, 'tok', axis=0, tiled=True)  77.4 us
    all_gather x1, waiting for transfers between devices, shards(): lax.all_gather(w_down, 'tok', axis=1, tiled=True)  73.9 us
    all_gather x1, waiting for transfers between devices, shards(): lax.all_gather(w_qkv, 'tok', axis=0, tiled=True)  67 us
    all_gather x1, blocking collectives, shards(): lax.all_gather(w_out_self, 'tok', axis=1, tiled=True)  54.8 us
    all_gather x1, blocking collectives, shards(): lax.all_gather(w_query_cross, 'tok', axis=0, tiled=True)  49.2 us
    all_gather x1, blocking collectives, shards(): lax.all_gather(w_out_cross, 'tok', axis=1, tiled=True)  48.2 us
    psum x3, waiting for transfers between devices, layer_sum(): lax.psum(summand.astype(jnp.bfloat16), 'grp').astype(jnp.float32)  44.3 us
    all_gather x1, waiting for transfers between devices, shards(): lax.all_gather(w_gate, 'tok', axis=0, tiled=True)  28.7 us
  transfers between devices with their start and end apart: 7, of which 5 were waited for; matrix products, arithmetic and copies ran while one was open for 4% of the time, Pallas kernels for 0%

commit v1 on v0

--- a/solution.py
+++ b/solution.py
@@ -4,6 +4,12 @@
 from jax.sharding import PartitionSpec as P
 
 DH = 64
+
+
+def _rest_sums_all(xx):
+    reached = jnp.stack([xx] * lax.axis_size("tok"), axis=0)
+    newest = lax.all_to_all(reached, "tok", 0, 0)
+    return jnp.concatenate(newest, axis=1)
 
 
 def ancestor_table(parent_ids):
@@ -120,7 +126,7 @@
     fetched = (
         lax.all_gather(w_out_self, "tok", axis=1, tiled=True),
         lax.all_gather(w_query_cross, "tok", axis=0, tiled=True),
-        lax.all_gather(w_out_cross, "tok", axis=1, tiled=True),
+        _rest_sums_all(w_out_cross),
         lax.all_gather(w_gate, "tok", axis=0, tiled=True),
         lax.all_gather(w_up, "tok", axis=0, tiled=True),
         lax.all_gather(w_down, "tok", axis=1, tiled=True),

time: 533 us -> 496 us (0.931)
  blocking collectives: 152 us -> 106 us
  starting transfers between devices: 0.55 us -> 6.96 us
    all_gather x1 -> x0, blocking collectives: 48.2 us -> none  [shards(): lax.all_gather(w_out_cross, 'tok', axis=1, tiled=True)]
    all_to_all x0 -> x1, starting transfers between devices: none -> 6.46 us  [_rest_sums_all(): newest = lax.all_to_all(reached, 'tok', 0, 0)]
  transfers between devices with their start and end apart: 7 -> 8, of which waited for: 5 -> 5; matrix products, arithmetic and copies ran while one was open for 4% -> 6% of each run, Pallas kernels for 0% -> 0%
where the time goes in v1:
time: 496 us; the launch traced here: 495 us
  waiting for transfers between devices  295 us (59%)
  blocking collectives  106 us (21%)
  local copies, waits for them, and re-layouts  34.2 us (7%)
  matrix products  24.9 us (5%)
  between operations  15.9 us (3%)
  other arithmetic  12.3 us (2%)
  starting transfers between devices  6.96 us (1%)
    all_gather x1, waiting for transfers between devices, shards(): lax.all_gather(w_up, 'tok', axis=0, tiled=True)  77.4 us
    all_gather x1, waiting for transfers between devices, shards(): lax.all_gather(w_down, 'tok', axis=1, tiled=True)  73.9 us
    all_gather x1, waiting for transfers between devices, shards(): lax.all_gather(w_qkv, 'tok', axis=0, tiled=True)  67.1 us
    all_gather x1, blocking collectives, shards(): lax.all_gather(w_out_self, 'tok', axis=1, tiled=True)  54.8 us
    all_gather x1, blocking collectives, shards(): lax.all_gather(w_query_cross, 'tok', axis=0, tiled=True)  51.2 us
    psum x3, waiting for transfers between devices, layer_sum(): lax.psum(summand.astype(jnp.bfloat16), 'grp').astype(jnp.float32)  45.1 us
    all_gather x1, waiting for transfers between devices, shards(): lax.all_gather(w_gate, 'tok', axis=0, tiled=True)  28.8 us
  transfers between devices with their start and end apart: 8, of which 5 were waited for; matrix products, arithmetic and copies ran while one was open for 6% of the time, Pallas kernels for 0%

profile of v1, /device:TPU:1, one launch (start us, length us, event | category | flops | bytes accessed | tf_op | source)
XLA Modules:
  0.0 494.9 jit_solution(7325701304435429074)
XLA Ops:
  8.1 3.9 fusion.55
  12.0 2.4 copy.55
  14.6 2.9 copy.49
  17.5 1.9 fusion.56
  19.7 3.6 fusion.1
  23.3 2.6 copy.54
  25.8 1.2 reshape_squeeze.23
  27.1 0.5 convolution_minimum_fusion.6
  27.6 0.4 convolution_minimum_fusion.5
  28.0 0.4 convolution_minimum_fusion.4
  28.4 0.4 convolution_minimum_fusion.3
  28.8 0.4 convolution_minimum_fusion.2
  29.2 0.4 convolution_minimum_fusion.1
  29.7 0.4 fusion.29
  30.3 0.8 fusion.3
  31.0 0.4 copy-done.3
  31.5 0.4 fusion.57
  31.9 1.5 fusion.7
  33.7 1.0 reshape_squeeze.25
  34.7 3.0 fusion.14
  37.8 0.4 fusion.27
  38.2 0.4 copy.58
  38.6 0.3 dot_general.79
  39.0 54.8 %all_gather.18 = bf16[256,1024]{0,1:T(8,128)(2,1)S(1)} all-gather(bf16[256,16]{0,1:T(8,128)(2,1)S(1)} %copy-done.9), channel_id=1, replica_groups=mesh['grp'=4,'tok'=64] {'tok'}, dimensions={1}, use_global_device_ids=true | all-gather | bytes 532480 | tf_op jit(solution)/shard_map/all_gather | solution.py:127
  93.8 0.5 fusion.31
  94.4 1.1 convert_element_type.84
  95.6 0.8 stack.2
  96.4 6.5 %all-to-all-start = ((bf16[64,256,16]{1,2,0:T(8,128)(2,1)}), bf16[64,256,16]{1,2,0:T(8,128)(2,1)S(1)}, u32[]{:S(2)}, u32[]{:S(2)}) async-start(bf16[64,256,16]{1,2,0:T(8,128)(2,1)} %stack.2), calls=%async_computation | async-start | bytes 1048576 | tf_op jit(solution)/shard_map/all_to_all | solution.py:11
  102.9 4.1 fusion.54
  107.0 2.4 copy.61
  109.4 2.9 copy.59
  112.3 51.2 %all_gather.19 = bf16[1024,256]{1,0:T(8,128)(2,1)S(1)} all-gather(bf16[16,256]{1,0:T(8,128)(2,1)S(1)} %copy-done.11), channel_id=1, replica_groups=mesh['grp'=4,'tok'=64] {'tok'}, dimensions={0}, use_global_device_ids=true | all-gather | bytes 532480 | tf_op jit(solution)/shard_map/all_gather | solution.py:128
  163.6 1.5 fusion.8
  165.1 1.5 fusion.10
  166.6 0.4 convolution_convert_fusion.3
  167.1 0.2 reshape_reshape.3
  167.3 0.7 fusion.33
  168.0 2.0 fusion.58
  170.0 0.8 fusion.26
  170.8 0.4 copy.62
  171.2 0.3 dot_general.84
  171.6 1.5 convolution_convert_fusion.1
  173.2 0.5 all-gather.5.cloned.1.call-update
  173.7 0.5 all-gather.9.cloned.1.call-update
  174.3 0.5 all-gather.7.cloned.1.call-update
  174.9 0.7 all-gather.11.cloned.1.call-update
  175.6 0.3 all-reduce.8.cloned.1.call-start
  175.9 45.1 %all-reduce.6.cloned.1.call-done = bf16[8,64,1024]{2,1,0:T(8,128)(2,1)} async-done(((bf16[8,64,1024]{2,1,0:T(8,128)(2,1)}), bf16[8,64,1024]{2,1,0:T(8,128)(2,1)}) %all-reduce.6.cloned.1.call-update) | async-done | bytes 1048592 | tf_op jit(solution)/shard_map/psum | solution.py:93
  221.0 1.7 multiply_reduce_fusion.1
  222.7 0.4 multiply_convert_fusion.1
  223.1 28.8 %all-gather.5.cloned.1.call-done = bf16[1024,704]{1,0:T(8,128)(2,1)} async-done(((bf16[16,704]{1,0:T(8,128)(2,1)}), bf16[1024,704]{1,0:T(8,128)(2,1)}) %all-gather.5.cloned.1.call-update) | async-done | bytes 1441808 | tf_op jit(solution)/shard_map/all_gather | solution.py:130
  251.9 3.5 fusion.59
  255.3 73.9 %all-gather.9.cloned.1.call-done = bf16[704,1024]{0,1:T(8,128)(2,1)} async-done(((bf16[704,16]{0,1:T(8,128)(2,1)}), bf16[704,1024]{0,1:T(8,128)(2,1)}) %all-gather.9.cloned.1.call-update) | async-done | bytes 1441808 | tf_op jit(solution)/shard_map/all_gather | solution.py:132
  329.3 77.4 %all-gather.7.cloned.1.call-done = bf16[1024,704]{1,0:T(8,128)(2,1)} async-done(((bf16[16,704]{1,0:T(8,128)(2,1)}), bf16[1024,704]{1,0:T(8,128)(2,1)}) %all-gather.7.cloned.1.call-update) | async-done | bytes 1441808 | tf_op jit(solution)/shard_map/all_gather | solution.py:131
  406.7 5.5 %convolution_convert_fusion = bf16[512,1024]{1,0:T(8,128)(2,1)} fusion(bf16[704,1024]{0,1:T(8,128)(2,1)} %all-gather.9.cloned.1.call-done, bf16[512,1024]{1,0:T(8,128)(2,1)S(1)} %bitcast.71, bf16[1024,704]{1,0:T(8,128)(2,1)} %all-gather.7.cloned.1.call-done, f32[512,704]{0,1:T(8,128)} %fusion.59), kind=kOutput, calls=%fused_computation.29 | convolution fusion | flops 1480523776 | bytes 6422528 | tf_op jit(solution)/shard_map/dot_general | solution.py:156
  412.2 67.1 %all-gather.11.cloned.1.call-done = bf16[1024,3,256]{2,0,1:T(8,128)(2,1)} async-done(((bf16[16,3,256]{2,0,1:T(8,128)(2,1)}), bf16[1024,3,256]{2,0,1:T(8,128)(2,1)}) %all-gather.11.cloned.1.call-update) | async-done | bytes 1572880 | tf_op jit(solution)/shard_map/all_gather | solution.py:133
  479.2 2.6 copy.64
  481.8 1.8 multiply_reduce_fusion
  483.6 0.7 dynamic-slice_convert_fusion
  484.3 0.2 multiply_convert_fusion
  484.6 0.5 copy-done.6
  485.1 1.0 convolution_convert_fusion.2
  486.1 0.4 reshape.151
  486.5 1.0 copy.65
  (66 shorter events, 1.6 us)
Async XLA Ops:
  8.0 155.6 %all-reduce.4.cloned.1.call-start = ((), (), s32[]{:S(2)}) async-start(), calls=%async_computation.1 | async-start | bytes 2097152 | tf_op jit(solution)/shard_map/psum | solution.py:93
  12.0 2.4 copy-start.16
  12.0 2.6 copy-start.17
  17.5 2.2 copy-start.19
  19.7 7.4 %copy-start.12 = (s32[8,64]{1,0:T(8,128)S(1)}, s32[8,64]{1,0:T(8,128)}, u32[]{:S(2)}) copy-start(s32[8,64]{1,0:T(8,128)} %param.24) | copy-start | bytes 6148
  27.1 2.5 copy-start.20
  30.2 1.2 copy-start.3
  31.5 2.0 copy-start.1
  31.9 2.8 copy-start.4
  34.7 3.1 copy-start.7
  37.8 1.2 copy-start.9
  38.6 55.7 %copy-start.8 = (bf16[8,16,1024]{2,1,0:T(8,128)(2,1)S(1)}, bf16[8,16,1024]{2,1,0:T(8,128)(2,1)}, u32[]{:S(2)}) copy-start(bf16[8,16,1024]{2,1,0:T(8,128)(2,1)} %param.20) | copy-start | bytes 786436
  94.4 1.2 copy-start.10
  96.4 75.1 %all-to-all-start = ((bf16[64,256,16]{1,2,0:T(8,128)(2,1)}), bf16[64,256,16]{1,2,0:T(8,128)(2,1)S(1)}, u32[]{:S(2)}, u32[]{:S(2)}) async-start(bf16[64,256,16]{1,2,0:T(8,128)(2,1)} %stack.2), calls=%async_computation | async-start | bytes 1048576 | tf_op jit(solution)/shard_map/all_to_all | solution.py:11
  102.9 118.1 %all-reduce.6.cloned.1.call-start = ((), (), s32[]{:S(2)}) async-start(), calls=%async_computation.2 | async-start | bytes 2097152 | tf_op jit(solution)/shard_map/psum | solution.py:93
  109.4 2.9 copy-start.11
  109.4 54.1 %copy-start.18 = (s32[8]{0:T(128)S(1)}, s32[8]{0:T(128)}, u32[]{:S(2)}) copy-start(s32[8]{0:T(128)} %param.27) | copy-start | bytes 100
  109.4 55.7 %copy-start.13 = (f32[1024]{0:T(1024)S(1)}, f32[1024]{0:T(1024)}, u32[]{:S(2)}) copy-start(f32[1024]{0:T(1024)} %param.30) | copy-start | bytes 12292
  168.0 2.0 copy-start.5
  171.2 49.8 %copy-start = (bf16[8,64,1024]{2,1,0:T(8,128)(2,1)S(1)}, bf16[8,64,1024]{2,1,0:T(8,128)(2,1)}, u32[]{:S(2)}) copy-start(bf16[8,64,1024]{2,1,0:T(8,128)(2,1)} %all-reduce.4.cloned.1.call-done) | copy-start | bytes 3145732
  171.6 51.2 %copy-start.14 = (f32[1024]{0:T(1024)S(1)}, f32[1024]{0:T(1024)}, u32[]{:S(2)}) copy-start(f32[1024]{0:T(1024)} %param.31) | copy-start | bytes 12292
  173.1 78.8 %all-gather.5.cloned.1.call-start = ((), (), s32[]{:S(2)}) async-start(), calls=%async_computation.3 | async-start | bytes 1597440 | tf_op jit(solution)/shard_map/all_gather | solution.py:130
  173.7 155.6 %all-gather.9.cloned.1.call-start = ((), (), s32[]{:S(2)}) async-start(), calls=%async_computation.5 | async-start | bytes 1597440 | tf_op jit(solution)/shard_map/all_gather | solution.py:132
  174.3 232.4 %all-gather.7.cloned.1.call-start = ((), (), s32[]{:S(2)}) async-start(), calls=%async_computation.4 | async-start | bytes 1597440 | tf_op jit(solution)/shard_map/all_gather | solution.py:131
  174.9 304.3 %all-gather.11.cloned.1.call-start = ((), (), s32[]{:S(2)}) async-start(), calls=%async_computation.7 | async-start | bytes 1597440 | tf_op jit(solution)/shard_map/all_gather | solution.py:133
  175.6 306.2 %all-reduce.8.cloned.1.call-start = ((), (), s32[]{:S(2)}) async-start(), calls=%async_computation.6 | async-start | bytes 2097152 | tf_op jit(solution)/shard_map/psum | solution.py:93
  221.0 1.7 copy-start.2
  481.8 2.5 copy-start.15
  483.6 1.5 copy-start.6
Sparse Core Ops, SparseCore 0:
  95.7 46.8 all-reduce.3
  173.2 47.6 all-reduce.5
  412.3 46.8 all-reduce.7
Sparse Core Ops, SparseCore 1:
  176.3 75.5 all-gather.4
  254.5 74.7 all-gather.8
  331.9 74.7 all-gather.6
  409.7 69.5 all-gather.10
